TPU v7x, 32 devices: a whole 2x2x4 slice. The times are simulated.
32 devices in a mesh: dp: 4 (over y, x), expert: 8 (over z, core).
Axes of the slice: x: 2, y: 2, z: 4, core: 2. Of those that a mesh axis runs over, the one named last changes fastest.
Arguments:
- features: float32 [32768, 256], P(('dp', 'expert')), may hold values from -6 to 6
- cotangent: float32 [32768, 512], P(('dp', 'expert')), may hold values from -6 to 6
- routes: int32 [32768, 8], P(('dp', 'expert')), may hold values from 0 to 15, all different within a row; in each aligned block of 256 rows (0 to 255, 256 to 511, ...) at most 192 rows name the same one
- lengths: int32 [32, 16], P(('dp', 'expert')), may hold values from 1 to 200, 1024 in all within a row
- gate_weight: float32 [256, 40], replicated, may hold values from -0.1875 to 0.1875
- first_weight: float32 [16, 256, 256], P('expert', 'dp'), may hold values from -0.375 to 0.375
- second_weight: float32 [16, 256, 256], P('expert', 'dp'), may hold values from -0.75 to 0.75
- expert_bias: float32 [16, 512], P('expert', 'dp'), may hold values from -0.625 to 0.625
- gate_momentum: float32 [256, 40], replicated, may hold values from -12 to 12
- gate_average: float32 [256, 40], replicated, may hold values from -0.1875 to 0.1875
- first_momentum: float32 [16, 256, 256], P('expert', 'dp'), may hold values from -1.25 to 1.25
- first_average: float32 [16, 256, 256], P('expert', 'dp'), may hold values from -0.375 to 0.375
- second_momentum: float32 [16, 256, 256], P('expert', 'dp'), may hold values from -0.625 to 0.625
- second_average: float32 [16, 256, 256], P('expert', 'dp'), may hold values from -0.75 to 0.75
- bias_momentum: float32 [16, 512], P('expert', 'dp'), may hold values from -1.25 to 1.25
- bias_average: float32 [16, 512], P('expert', 'dp'), may hold values from -0.625 to 0.625
Outputs:
- task_outputs: float32 [32768, 512], P(('dp', 'expert'))
- input_grad: float32 [32768, 256], P(('dp', 'expert'))
- gate_momentum_new: float32 [256, 40], replicated
- gate_weight_new: float32 [256, 40], replicated
- gate_average_new: float32 [256, 40], replicated
- first_momentum_new: float32 [16, 256, 256], P('expert', 'dp')
- first_weight_new: float32 [16, 256, 256], P('expert', 'dp')
- first_average_new: float32 [16, 256, 256], P('expert', 'dp')
- second_momentum_new: float32 [16, 256, 256], P('expert', 'dp')
- second_weight_new: float32 [16, 256, 256], P('expert', 'dp')
- second_average_new: float32 [16, 256, 256], P('expert', 'dp')
- bias_momentum_new: float32 [16, 512], P('expert', 'dp')
- bias_new: float32 [16, 512], P('expert', 'dp')
- bias_average_new: float32 [16, 512], P('expert', 'dp')
Inputs may be any that keep to these rules, and one draw needn't show every extreme that they name: `routes`: each row names 8 different experts: the first 4 are task 0's selectors, the next 4 task 1's. In each aligned block of 256 rows (one micro-batch of one device) no expert is named by more than 192 rows, and in some block one expert is named by exactly 192 rows. `lengths`: the sessions of one device cover its 1024 rows in order and never cross devices; the longest has the maximum length.
All inputs are finite; a program needn't handle non-finite values.
Results may differ from a plain program's by a relative error of at most 0.002.
Values sent between devices are 32-bit elements; how exact they have to be, the bound alone decides.
A program may use at most 192 MiB of HBM per device.

v0:
```python
import math
import jax
import jax.numpy as jnp
from jax import lax
from jax.sharding import PartitionSpec as P

D = 256
HID = 256
DOUT = 256
EXPERTS = 16
BITS = 4
TASKS = 2
SELECT = 4
MICRO = 4
CAP = 192
HIGHEST = lax.Precision.HIGHEST
OFFSET = 3.5
SHARPNESS = 10.0
MOMENTUM = 0.5
AVERAGE_DECAY = 0.5
EXPERT_RATE = 0.4
GATE_RATE = 0.01


def smooth_step(argument):
    clipped = jnp.clip(argument, -0.5 * SHARPNESS, 0.5 * SHARPNESS)
    return -2.0 / SHARPNESS**3 * clipped**3 + 1.5 / SHARPNESS * clipped + 0.5


def gate_strengths(features, gate_weight, lengths_row, chosen):
    row_count = features.shape[0]
    session_ends = jnp.cumsum(lengths_row, dtype=jnp.int32)
    starts = session_ends - lengths_row
    places = jnp.arange(row_count, dtype=jnp.int32)[:, None]
    member = ((places >= starts[None, :]) & (places < session_ends[None, :])).astype(jnp.float32)
    session_sums = jnp.dot(member.T, features, precision=HIGHEST)
    session_means = session_sums / lengths_row.astype(jnp.float32)[:, None]
    context = features + jnp.dot(member, session_means, precision=HIGHEST)
    logits = jnp.dot(context, gate_weight, precision=HIGHEST).reshape(
        row_count, TASKS, SELECT, BITS + 1
    )
    weights = jax.nn.softmax(logits[..., 0], axis=-1)
    powers = 2 ** jnp.arange(BITS, dtype=jnp.int32)
    code_bits = chosen.reshape(row_count, TASKS, SELECT)[..., None] // powers % 2
    code_signs = 2.0 * code_bits.astype(jnp.float32) - 1.0
    strength = jnp.prod(smooth_step(code_signs * logits[..., 1:] + OFFSET), axis=-1)
    return (weights * strength).reshape(row_count, TASKS * SELECT)


def slot_index(chosen):
    destination = chosen.reshape(-1)
    matches = (destination[:, None] == jnp.arange(EXPERTS, dtype=jnp.int32)[None, :]).astype(
        jnp.int32
    )
    before = jnp.cumsum(matches, axis=0, dtype=jnp.int32) - matches
    position = jnp.sum(before * matches, axis=1, dtype=jnp.int32)
    return destination * CAP + position


def expert_forward(slot_rows, first_full, second_full, bias_full):
    pre_act = (
        jnp.einsum("sjcd,jdh->sjch", slot_rows, first_full, precision=HIGHEST)
        + bias_full[None, :, None, :HID]
    )
    hidden = jax.nn.relu(pre_act)
    slot_out = (
        jnp.einsum("sjch,jho->sjco", hidden, second_full, precision=HIGHEST)
        + bias_full[None, :, None, HID:]
    )
    return (pre_act, hidden, slot_out)


def expert_backward(slot_rows, pre_act, hidden, slot_cot, first_full, second_full):
    second_delta = jnp.einsum("sjch,sjco->jho", hidden, slot_cot, precision=HIGHEST)
    hidden_cot = jnp.einsum("sjco,jho->sjch", slot_cot, second_full, precision=HIGHEST) * (
        pre_act > 0.0
    ).astype(jnp.float32)
    first_delta = jnp.einsum("sjcd,sjch->jdh", slot_rows, hidden_cot, precision=HIGHEST)
    bias_delta = jnp.concatenate(
        [jnp.sum(hidden_cot, axis=(0, 2)), jnp.sum(slot_cot, axis=(0, 2))], axis=-1
    )
    slot_back = jnp.einsum("sjch,jdh->sjcd", hidden_cot, first_full, precision=HIGHEST)
    return (slot_back, (first_delta, second_delta, bias_delta))


def apply_update(weight, gradient, momentum, average, step_rate):
    momentum_new = MOMENTUM * momentum + gradient
    weight_new = weight - step_rate * (gradient + MOMENTUM * momentum_new)
    average_new = AVERAGE_DECAY * average + (1.0 - AVERAGE_DECAY) * weight_new
    return (momentum_new, weight_new, average_new)


def local(
    features,
    cotangent,
    routes,
    lengths,
    gate_weight,
    first_weight,
    second_weight,
    expert_bias,
    gate_momentum,
    gate_average,
    first_momentum,
    first_average,
    second_momentum,
    second_average,
    bias_momentum,
    bias_average,
):
    row_count = features.shape[0]
    pair_count = TASKS * SELECT
    micro_rows = row_count // MICRO

    def gate_part(rows_in, weight_in):
        return gate_strengths(rows_in, weight_in, lengths[0], routes)

    gate_terms, gate_pull = jax.vjp(gate_part, features, gate_weight)
    pair_cot = jnp.broadcast_to(
        cotangent.reshape(row_count, TASKS, 1, DOUT), (row_count, TASKS, SELECT, DOUT)
    ).reshape(row_count, pair_count, DOUT)
    pair_grads = gate_terms[:, :, None] * pair_cot
    local_count = first_weight.shape[0]
    first_sum = jnp.zeros((local_count, D, HID), jnp.float32)
    second_sum = jnp.zeros((local_count, HID, DOUT), jnp.float32)
    bias_sum = jnp.zeros((local_count, HID + DOUT), jnp.float32)
    output_parts = []
    input_parts = []
    cot_parts = []
    for micro_index in range(MICRO):
        begin = micro_index * micro_rows
        first_full = lax.all_gather(first_weight, "dp", axis=1, tiled=True)
        second_full = lax.all_gather(second_weight, "dp", axis=1, tiled=True)
        bias_full = lax.all_gather(expert_bias, "dp", axis=1, tiled=True)
        rows_now = features[begin : begin + micro_rows]
        slot_place = slot_index(routes[begin : begin + micro_rows])
        send_rows = (
            jnp.zeros((EXPERTS * CAP, D), jnp.float32)
            .at[slot_place]
            .set(jnp.repeat(rows_now, pair_count, axis=0))
            .reshape(EXPERTS, CAP, D)
        )
        send_grads = (
            jnp.zeros((EXPERTS * CAP, DOUT), jnp.float32)
            .at[slot_place]
            .set(pair_grads[begin : begin + micro_rows].reshape(-1, DOUT))
            .reshape(EXPERTS, CAP, DOUT)
        )
        got_rows = lax.all_to_all(send_rows, "expert", split_axis=0, concat_axis=0, tiled=True)
        slot_rows = got_rows.reshape(-1, local_count, CAP, D)
        pre_act, hidden, slot_out = expert_forward(slot_rows, first_full, second_full, bias_full)
        returned_out = lax.all_to_all(
            slot_out.reshape(EXPERTS, CAP, DOUT), "expert", split_axis=0, concat_axis=0, tiled=True
        )
        got_grads = lax.all_to_all(send_grads, "expert", split_axis=0, concat_axis=0, tiled=True)
        slot_back, deltas = expert_backward(
            slot_rows,
            pre_act,
            hidden,
            got_grads.reshape(-1, local_count, CAP, DOUT),
            first_full,
            second_full,
        )
        returned_back = lax.all_to_all(
            slot_back.reshape(EXPERTS, CAP, D), "expert", split_axis=0, concat_axis=0, tiled=True
        )
        first_sum = first_sum + deltas[0]
        second_sum = second_sum + deltas[1]
        bias_sum = bias_sum + deltas[2]
        picked = returned_out.reshape(EXPERTS * CAP, DOUT)[slot_place].reshape(
            micro_rows, TASKS, SELECT, DOUT
        )
        combined = jnp.sum(
            gate_terms[begin : begin + micro_rows].reshape(micro_rows, TASKS, SELECT, 1) * picked,
            axis=2,
        )
        output_parts.append(combined.reshape(micro_rows, TASKS * DOUT))
        cot_parts.append(
            jnp.sum(
                pair_cot[begin : begin + micro_rows] * picked.reshape(micro_rows, pair_count, DOUT),
                axis=-1,
            )
        )
        input_parts.append(
            jnp.sum(
                returned_back.reshape(EXPERTS * CAP, D)[slot_place].reshape(
                    micro_rows, pair_count, D
                ),
                axis=1,
            )
        )
    task_outputs = jnp.concatenate(output_parts, axis=0)
    rows_from_gate, gate_local = gate_pull(jnp.concatenate(cot_parts, axis=0))
    input_grad = rows_from_gate + jnp.concatenate(input_parts, axis=0)
    gate_grad = lax.psum(gate_local, ("dp", "expert"))
    first_grad, second_grad, bias_grad = (
        lax.psum_scatter(first_sum, "dp", scatter_dimension=1, tiled=True),
        lax.psum_scatter(second_sum, "dp", scatter_dimension=1, tiled=True),
        lax.psum_scatter(bias_sum, "dp", scatter_dimension=1, tiled=True),
    )
    grad_scale = 1.0 / math.sqrt(row_count * lax.axis_size("dp") * lax.axis_size("expert"))
    gate_new = apply_update(
        gate_weight, gate_grad * grad_scale, gate_momentum, gate_average, GATE_RATE
    )
    first_new = apply_update(
        first_weight, first_grad * grad_scale, first_momentum, first_average, EXPERT_RATE
    )
    second_new = apply_update(
        second_weight, second_grad * grad_scale, second_momentum, second_average, EXPERT_RATE
    )
    bias_new = apply_update(
        expert_bias, bias_grad * grad_scale, bias_momentum, bias_average, EXPERT_RATE
    )
    return (
        task_outputs,
        input_grad,
        gate_new[0],
        gate_new[1],
        gate_new[2],
        first_new[0],
        first_new[1],
        first_new[2],
        second_new[0],
        second_new[1],
        second_new[2],
        bias_new[0],
        bias_new[1],
        bias_new[2],
    )


def solution(mesh):
    placed = (
        P(("dp", "expert"), None),
        P(("dp", "expert"), None),
        P(("dp", "expert"), None),
        P(("dp", "expert"), None),
        P(),
        P("expert", "dp", None),
        P("expert", "dp", None),
        P("expert", "dp"),
        P(),
        P(),
        P("expert", "dp", None),
        P("expert", "dp", None),
        P("expert", "dp", None),
        P("expert", "dp", None),
        P("expert", "dp"),
        P("expert", "dp"),
    )
    return jax.shard_map(
        local,
        mesh=mesh,
        in_specs=placed,
        out_specs=(
            P(("dp", "expert"), None),
            P(("dp", "expert"), None),
            P(),
            P(),
            P(),
            P("expert", "dp", None),
            P("expert", "dp", None),
            P("expert", "dp", None),
            P("expert", "dp", None),
            P("expert", "dp", None),
            P("expert", "dp", None),
            P("expert", "dp"),
            P("expert", "dp"),
            P("expert", "dp"),
        ),
        check_vma=False,
    )
```

profile of v0, /device:TPU:0, one launch (start us, length us, event | category | flops | bytes accessed | tf_op | source)
XLA Modules:
  0.0 1447.1 jit_solution(313344892652982760)
XLA Ops:
  16.6 10.9 scatter_custom_fusion
  53.4 11.3 scatter_custom_fusion.3
  64.7 40.7 %all-to-all-done = f32[16,192,256]{2,1,0:T(8,128)S(1)} async-done(((f32[16,192,256]{2,1,0:T(8,128)}), f32[16,192,256]{2,1,0:T(8,128)S(1)}, u32[]{:S(2)}, u32[]{:S(2)}) %all-to-all-start) | async-done | bytes 3145760 | tf_op jit(solution)/shard_map/all_to_all | solution.py:149
  130.3 11.2 scatter_custom_fusion.2
  141.6 40.6 %all-to-all-done.6 = f32[16,192,256]{2,1,0:T(8,128)S(1)} async-done(((f32[16,192,256]{2,1,0:T(8,128)}), f32[16,192,256]{2,1,0:T(8,128)S(1)}, u32[]{:S(2)}, u32[]{:S(2)}) %all-to-all-start.6) | async-done | bytes 3145760 | tf_op jit(solution)/shard_map/all_to_all | solution.py:149
  194.5 10.9 scatter_custom_fusion.1
  205.4 54.6 %all-to-all-done.4 = f32[16,192,256]{2,1,0:T(8,128)} async-done(((f32[16,192,256]{2,1,0:T(8,128)}), f32[16,192,256]{2,1,0:T(8,128)}, u32[]{:S(2)}, u32[]{:S(2)}) %all-to-all-start.4) | async-done | bytes 3145760 | tf_op jit(solution)/shard_map/all_to_all | solution.py:149
  272.0 10.7 all_gather.6
  302.2 33.1 %all-to-all-done.2 = f32[16,192,256]{2,1,0:T(8,128)S(1)} async-done(((f32[16,192,256]{2,1,0:T(8,128)}), f32[16,192,256]{2,1,0:T(8,128)S(1)}, u32[]{:S(2)}, u32[]{:S(2)}) %all-to-all-start.2) | async-done | bytes 3145760 | tf_op jit(solution)/shard_map/all_to_all | solution.py:149
  351.1 61.2 %all-to-all-done.1 = f32[16,192,256]{2,1,0:T(8,128)S(1)} async-done(((f32[16,192,256]{2,1,0:T(8,128)}), f32[16,192,256]{2,1,0:T(8,128)S(1)}, u32[]{:S(2)}, u32[]{:S(2)}) %all-to-all-start.1) | async-done | bytes 3145760 | tf_op jit(solution)/shard_map/all_to_all | solution.py:152
  427.6 61.2 %all-to-all-done.7 = f32[16,192,256]{2,1,0:T(8,128)} async-done(((f32[16,192,256]{2,1,0:T(8,128)}), f32[16,192,256]{2,1,0:T(8,128)}, u32[]{:S(2)}, u32[]{:S(2)}) %all-to-all-start.7) | async-done | bytes 3145760 | tf_op jit(solution)/shard_map/all_to_all | solution.py:152
  503.7 61.3 %all-to-all-done.5 = f32[16,192,256]{2,1,0:T(8,128)} async-done(((f32[16,192,256]{2,1,0:T(8,128)}), f32[16,192,256]{2,1,0:T(8,128)}, u32[]{:S(2)}, u32[]{:S(2)}) %all-to-all-start.5) | async-done | bytes 3145760 | tf_op jit(solution)/shard_map/all_to_all | solution.py:152
  698.7 11.5 scatter_custom_fusion.7
  715.7 11.5 scatter_custom_fusion.6
  727.2 60.0 %all-to-all-done.14 = f32[16,192,256]{2,1,0:T(8,128)S(1)} async-done(((f32[16,192,256]{2,1,0:T(8,128)}), f32[16,192,256]{2,1,0:T(8,128)S(1)}, u32[]{:S(2)}, u32[]{:S(2)}) %all-to-all-start.14) | async-done | bytes 3145760 | tf_op jit(solution)/shard_map/all_to_all | solution.py:155
  793.5 11.4 scatter_custom_fusion.5
  804.9 60.1 %all-to-all-done.12 = f32[16,192,256]{2,1,0:T(8,128)} async-done(((f32[16,192,256]{2,1,0:T(8,128)}), f32[16,192,256]{2,1,0:T(8,128)}, u32[]{:S(2)}, u32[]{:S(2)}) %all-to-all-start.12) | async-done | bytes 3145760 | tf_op jit(solution)/shard_map/all_to_all | solution.py:155
  868.7 11.5 scatter_custom_fusion.4
  880.2 60.0 %all-to-all-done.10 = f32[16,192,256]{2,1,0:T(8,128)S(1)} async-done(((f32[16,192,256]{2,1,0:T(8,128)}), f32[16,192,256]{2,1,0:T(8,128)S(1)}, u32[]{:S(2)}, u32[]{:S(2)}) %all-to-all-start.10) | async-done | bytes 3145760 | tf_op jit(solution)/shard_map/all_to_all | solution.py:155
  957.4 60.8 %all-to-all-done.8 = f32[16,192,256]{2,1,0:T(8,128)} async-done(((f32[16,192,256]{2,1,0:T(8,128)}), f32[16,192,256]{2,1,0:T(8,128)}, u32[]{:S(2)}, u32[]{:S(2)}) %all-to-all-start.8) | async-done | bytes 3145760 | tf_op jit(solution)/shard_map/all_to_all | solution.py:155
  1033.9 59.7 %all-to-all-done.15 = f32[16,192,256]{2,1,0:T(8,128)S(1)} async-done(((f32[16,192,256]{2,1,0:T(8,128)}), f32[16,192,256]{2,1,0:T(8,128)S(1)}, u32[]{:S(2)}, u32[]{:S(2)}) %all-to-all-start.15) | async-done | bytes 3145760 | tf_op jit(solution)/shard_map/all_to_all | solution.py:164
  1110.0 59.8 %all-to-all-done.13 = f32[16,192,256]{2,1,0:T(8,128)} async-done(((f32[16,192,256]{2,1,0:T(8,128)}), f32[16,192,256]{2,1,0:T(8,128)}, u32[]{:S(2)}, u32[]{:S(2)}) %all-to-all-start.13) | async-done | bytes 3145760 | tf_op jit(solution)/shard_map/all_to_all | solution.py:164
  1243.9 41.1 %psum.7 = f32[256,40]{0,1:T(8,128)S(1)} all-reduce(f32[256,40]{0,1:T(8,128)S(1)} %fusion.258), channel_id=1, replica_groups=mesh['dp'=4,'expert'=8] {'dp','expert'}, use_global_device_ids=true, to_apply=%region_36.37 | all-reduce | flops 10240 | bytes 81920 | tf_op jit(solution)/shard_map/psum | solution.py:195
  1374.8 17.6 %reduce-scatter.6.cloned.1.call-done = f32[2,64,256]{2,1,0:T(8,128)} async-done(((f32[2,256,256]{2,1,0:T(8,128)}), f32[2,64,256]{2,1,0:T(8,128)}) %reduce-scatter.6.cloned.1.call-update) | async-done | bytes 131088 | tf_op jit(solution)/shard_map/reduce_scatter | solution.py:197
  (429 shorter events, 558.6 us)
Async XLA Ops:
  27.5 77.9 %all-to-all-start = ((f32[16,192,256]{2,1,0:T(8,128)}), f32[16,192,256]{2,1,0:T(8,128)S(1)}, u32[]{:S(2)}, u32[]{:S(2)}) async-start(f32[16,192,256]{2,1,0:T(8,128)} %bitcast.394), calls=%async_computation | async-start | bytes 6291456 | tf_op jit(solution)/shard_map/all_to_all | solution.py:149
  53.4 53.7 %copy-start.71 = (s32[2048,1]{0,1:T(1,128)}, s32[2048,1]{0,1:T(1,128)S(1)}, u32[]{:S(2)}) copy-start(s32[2048,1]{0,1:T(1,128)S(1)} %compare_select_fusion) | copy-start | bytes 24580
  107.1 75.1 %all-to-all-start.6 = ((f32[16,192,256]{2,1,0:T(8,128)}), f32[16,192,256]{2,1,0:T(8,128)S(1)}, u32[]{:S(2)}, u32[]{:S(2)}) async-start(f32[16,192,256]{2,1,0:T(8,128)} %bitcast.393), calls=%async_computation.6 | async-start | bytes 6291456 | tf_op jit(solution)/shard_map/all_to_all | solution.py:149
  130.3 51.9 %copy-start.73 = (s32[2048,1]{0,1:T(1,128)}, s32[2048,1]{0,1:T(1,128)S(1)}, u32[]{:S(2)}) copy-start(s32[2048,1]{0,1:T(1,128)S(1)} %compare_select_fusion.1) | copy-start | bytes 24580
  183.9 76.2 %all-to-all-start.4 = ((f32[16,192,256]{2,1,0:T(8,128)}), f32[16,192,256]{2,1,0:T(8,128)}, u32[]{:S(2)}, u32[]{:S(2)}) async-start(f32[16,192,256]{2,1,0:T(8,128)} %bitcast.392), calls=%async_computation.4 | async-start | bytes 6291456 | tf_op jit(solution)/shard_map/all_to_all | solution.py:149
  194.5 65.6 %copy-start.75 = (s32[2048,1]{0,1:T(1,128)}, s32[2048,1]{0,1:T(1,128)S(1)}, u32[]{:S(2)}) copy-start(s32[2048,1]{0,1:T(1,128)S(1)} %compare_select_fusion.2) | copy-start | bytes 24580
  260.1 22.6 %copy-start.43 = (f32[2,64,256]{2,1,0:T(8,128)S(1)}, f32[2,64,256]{2,1,0:T(8,128)}, u32[]{:S(2)}) copy-start(f32[2,64,256]{2,1,0:T(8,128)} %param.22) | copy-start | bytes 393220
  260.1 75.3 %all-to-all-start.2 = ((f32[16,192,256]{2,1,0:T(8,128)}), f32[16,192,256]{2,1,0:T(8,128)S(1)}, u32[]{:S(2)}, u32[]{:S(2)}) async-start(f32[16,192,256]{2,1,0:T(8,128)} %bitcast.395), calls=%async_computation.2 | async-start | bytes 6291456 | tf_op jit(solution)/shard_map/all_to_all | solution.py:149
  337.0 75.4 %all-to-all-start.1 = ((f32[16,192,256]{2,1,0:T(8,128)}), f32[16,192,256]{2,1,0:T(8,128)S(1)}, u32[]{:S(2)}, u32[]{:S(2)}) async-start(f32[16,192,256]{2,1,0:T(8,128)} %bitcast.399), calls=%async_computation.1 | async-start | bytes 6291456 | tf_op jit(solution)/shard_map/all_to_all | solution.py:152
  412.3 76.5 %all-to-all-start.7 = ((f32[16,192,256]{2,1,0:T(8,128)}), f32[16,192,256]{2,1,0:T(8,128)}, u32[]{:S(2)}, u32[]{:S(2)}) async-start(f32[16,192,256]{2,1,0:T(8,128)} %bitcast.400), calls=%async_computation.7 | async-start | bytes 6291456 | tf_op jit(solution)/shard_map/all_to_all | solution.py:152
  488.8 76.2 %all-to-all-start.5 = ((f32[16,192,256]{2,1,0:T(8,128)}), f32[16,192,256]{2,1,0:T(8,128)}, u32[]{:S(2)}, u32[]{:S(2)}) async-start(f32[16,192,256]{2,1,0:T(8,128)} %bitcast.398), calls=%async_computation.5 | async-start | bytes 6291456 | tf_op jit(solution)/shard_map/all_to_all | solution.py:152
  565.0 114.0 %all-to-all-start.3 = ((f32[16,192,256]{2,1,0:T(8,128)}), f32[16,192,256]{2,1,0:T(8,128)}, u32[]{:S(2)}, u32[]{:S(2)}) async-start(f32[16,192,256]{2,1,0:T(8,128)} %bitcast.391), calls=%async_computation.3 | async-start | bytes 6291456 | tf_op jit(solution)/shard_map/all_to_all | solution.py:152
  710.2 77.1 %all-to-all-start.14 = ((f32[16,192,256]{2,1,0:T(8,128)}), f32[16,192,256]{2,1,0:T(8,128)S(1)}, u32[]{:S(2)}, u32[]{:S(2)}) async-start(f32[16,192,256]{2,1,0:T(8,128)} %bitcast.404), calls=%async_computation.14 | async-start | bytes 6291456 | tf_op jit(solution)/shard_map/all_to_all | solution.py:155
  789.0 76.0 %all-to-all-start.12 = ((f32[16,192,256]{2,1,0:T(8,128)}), f32[16,192,256]{2,1,0:T(8,128)}, u32[]{:S(2)}, u32[]{:S(2)}) async-start(f32[16,192,256]{2,1,0:T(8,128)} %bitcast.403), calls=%async_computation.12 | async-start | bytes 6291456 | tf_op jit(solution)/shard_map/all_to_all | solution.py:155
  865.0 75.1 %all-to-all-start.10 = ((f32[16,192,256]{2,1,0:T(8,128)}), f32[16,192,256]{2,1,0:T(8,128)S(1)}, u32[]{:S(2)}, u32[]{:S(2)}) async-start(f32[16,192,256]{2,1,0:T(8,128)} %bitcast.402), calls=%async_computation.10 | async-start | bytes 6291456 | tf_op jit(solution)/shard_map/all_to_all | solution.py:155
  941.8 76.4 %all-to-all-start.8 = ((f32[16,192,256]{2,1,0:T(8,128)}), f32[16,192,256]{2,1,0:T(8,128)}, u32[]{:S(2)}, u32[]{:S(2)}) async-start(f32[16,192,256]{2,1,0:T(8,128)} %bitcast.401), calls=%async_computation.8 | async-start | bytes 6291456 | tf_op jit(solution)/shard_map/all_to_all | solution.py:155
  1018.2 75.3 %all-to-all-start.15 = ((f32[16,192,256]{2,1,0:T(8,128)}), f32[16,192,256]{2,1,0:T(8,128)S(1)}, u32[]{:S(2)}, u32[]{:S(2)}) async-start(f32[16,192,256]{2,1,0:T(8,128)} %bitcast.396), calls=%async_computation.15 | async-start | bytes 6291456 | tf_op jit(solution)/shard_map/all_to_all | solution.py:164
  1093.5 76.2 %all-to-all-start.13 = ((f32[16,192,256]{2,1,0:T(8,128)}), f32[16,192,256]{2,1,0:T(8,128)}, u32[]{:S(2)}, u32[]{:S(2)}) async-start(f32[16,192,256]{2,1,0:T(8,128)} %bitcast.397), calls=%async_computation.13 | async-start | bytes 6291456 | tf_op jit(solution)/shard_map/all_to_all | solution.py:164
  1169.7 126.5 %all-to-all-start.11 = ((f32[16,192,256]{2,1,0:T(8,128)}), f32[16,192,256]{2,1,0:T(8,128)}, u32[]{:S(2)}, u32[]{:S(2)}) async-start(f32[16,192,256]{2,1,0:T(8,128)} %bitcast.390), calls=%async_computation.11 | async-start | bytes 6291456 | tf_op jit(solution)/shard_map/all_to_all | solution.py:164
  1296.3 132.1 %all-to-all-start.9 = ((f32[16,192,256]{2,1,0:T(8,128)}), f32[16,192,256]{2,1,0:T(8,128)}, u32[]{:S(2)}, u32[]{:S(2)}) async-start(f32[16,192,256]{2,1,0:T(8,128)} %bitcast.389), calls=%async_computation.9 | async-start | bytes 6291456 | tf_op jit(solution)/shard_map/all_to_all | solution.py:164
  1300.9 70.6 %reduce-scatter.10.cloned.1.call-start = ((), (), s32[]{:S(2)}) async-start(), calls=%async_computation.21 | async-start | bytes 327680
  1311.2 61.8 %reduce-scatter.8.cloned.1.call-start = ((), (), s32[]{:S(2)}) async-start(), calls=%async_computation.20 | async-start | bytes 655360 | tf_op jit(solution)/shard_map/reduce_scatter | solution.py:198
  1338.7 53.7 %reduce-scatter.6.cloned.1.call-start = ((), (), s32[]{:S(2)}) async-start(), calls=%async_computation.19 | async-start | bytes 655360 | tf_op jit(solution)/shard_map/reduce_scatter | solution.py:197
  1368.9 25.4 %copy-start.66 = (s32[2048]{0:T(1024)S(1)}, s32[2048]{0:T(1024)}, u32[]{:S(2)}) copy-start(s32[2048]{0:T(1024)} %broadcast_clamp_fusion) | copy-start | bytes 24580
  (86 other events, 501.4 us)
Sparse Core Ops, SparseCore 0:
  1311.3 25.2 reduce-scatter.9
  1339.7 25.0 reduce-scatter.7
  1367.6 24.7 reduce-scatter.5
where the time goes:
time: 1460 us; the launch traced here: 1450 us
  waiting for transfers between devices  731 us (50%)
  local copies, waits for them, and re-layouts  319 us (22%)
  matrix products  135 us (9%)
  other arithmetic  104 us (7%)
  starting transfers between devices  73.8 us (5%)
  blocking collectives  69.1 us (5%)
  between operations  15.8 us (1%)
    all_to_all x4, waiting for transfers between devices, local(): lax.all_to_all(send_grads, 'expert', split_axis=0, concat_axis=0, tiled=T...  241 us
    all_to_all x4, waiting for transfers between devices, local(): lax.all_to_all(slot_out.reshape(EXPERTS, CAP, DOUT), 'expert', split_axis...  184 us
    all_to_all x4, waiting for transfers between devices, local(): lax.all_to_all(send_rows, 'expert', split_axis=0, concat_axis=0, tiled=True)  169 us
    all_to_all x4, waiting for transfers between devices, local(): lax.all_to_all(slot_back.reshape(EXPERTS, CAP, D), 'expert', split_axis=0...  119 us
    scatter x4, local copies, waits for them, and re-layouts, local(): send_grads = jnp.zeros((EXPERTS * CAP, DOUT), jnp.float32).at[slot_place]...  45.9 us
    scatter x4, local copies, waits for them, and re-layouts, local(): send_rows = jnp.zeros((EXPERTS * CAP, D), jnp.float32).at[slot_place].set...  44.3 us
    psum x1, blocking collectives, local(): gate_grad = lax.psum(gate_local, ('dp', 'expert'))  41.1 us
    gather x4, local copies, waits for them, and re-layouts, local(): returned_back.reshape(EXPERTS * CAP, D)[slot_place]  38.5 us
  transfers between devices with their start and end apart: 19, of which 14 were waited for; matrix products, arithmetic and copies ran while one was open for 33% of the time, Pallas kernels for 0%

commit v1 on v0

--- a/solution.py
+++ b/solution.py
@@ -146,7 +146,20 @@
             .set(pair_grads[begin : begin + micro_rows].reshape(-1, DOUT))
             .reshape(EXPERTS, CAP, DOUT)
         )
-        got_rows = lax.all_to_all(send_rows, "expert", split_axis=0, concat_axis=0, tiled=True)
+        ways, here = (lax.axis_size("expert"), lax.axis_index("expert"))
+        width = send_rows.shape[0] // ways
+        lengths_2 = list(send_rows.shape)
+        lengths_2[0] = width
+        height = lengths_2[0]
+        lengths_2[0] = height * ways
+        got_rows = jnp.zeros(lengths_2, send_rows.dtype)
+        for mask in range(ways):
+            part = lax.dynamic_slice_in_dim(send_rows, (here ^ mask) * width, width, axis=0)
+            if mask:
+                part = lax.ppermute(part, "expert", [(d, d ^ mask) for d in range(ways)])
+            got_rows = lax.dynamic_update_slice_in_dim(
+                got_rows, part, (here ^ mask) * height, axis=0
+            )
         slot_rows = got_rows.reshape(-1, local_count, CAP, D)
         pre_act, hidden, slot_out = expert_forward(slot_rows, first_full, second_full, bias_full)
         returned_out = lax.all_to_all(

time: 1460 us -> 1450 us (level)
  starting transfers between devices: 73.8 us -> 128 us
  waiting for transfers between devices: 731 us -> 697 us
    ppermute x0 -> x28, waiting for transfers between devices: none -> 317 us  [local(): part = lax.ppermute(part, 'expert', [(d, d ^ mask) for d in range(ways)])]
    all_to_all x4, waiting for transfers between devices: 184 us -> 0.01 us  [local(): lax.all_to_all(slot_out.reshape(EXPERTS, CAP, DOUT), 'expert', split_axis...]
    all_to_all x4 -> x0, waiting for transfers between devices: 169 us -> none  [local(): lax.all_to_all(send_rows, 'expert', split_axis=0, concat_axis=0, tiled=True)]
    ppermute x0 -> x28, starting transfers between devices: none -> 46.5 us  [local(): part = lax.ppermute(part, 'expert', [(d, d ^ mask) for d in range(ways)])]
    all_to_all x4, starting transfers between devices: 18.3 us -> 44.2 us  [local(): lax.all_to_all(slot_out.reshape(EXPERTS, CAP, DOUT), 'expert', split_axis...]
    all_to_all x4 -> x0, starting transfers between devices: 18.4 us -> none  [local(): lax.all_to_all(send_rows, 'expert', split_axis=0, concat_axis=0, tiled=True)]
  transfers between devices with their start and end apart: 19 -> 43, of which waited for: 14 -> 21; matrix products, arithmetic and copies ran while one was open for 33% -> 31% of each run, Pallas kernels for 0% -> 0%
where the time goes in v1:
time: 1450 us; the launch traced here: 1440 us
  waiting for transfers between devices  697 us (48%)
  local copies, waits for them, and re-layouts  312 us (22%)
  starting transfers between devices  128 us (9%)
  matrix products  127 us (9%)
  other arithmetic  94.3 us (7%)
  blocking collectives  69.5 us (5%)
  between operations  16.1 us (1%)
    ppermute x28, waiting for transfers between devices, local(): part = lax.ppermute(part, 'expert', [(d, d ^ mask) for d in range(ways)])  317 us
    all_to_all x4, waiting for transfers between devices, local(): lax.all_to_all(send_grads, 'expert', split_axis=0, concat_axis=0, tiled=T...  241 us
    all_to_all x4, waiting for transfers between devices, local(): lax.all_to_all(slot_back.reshape(EXPERTS, CAP, D), 'expert', split_axis=0...  119 us
    ppermute x28, starting transfers between devices, local(): part = lax.ppermute(part, 'expert', [(d, d ^ mask) for d in range(ways)])  46.5 us
    scatter x4, local copies, waits for them, and re-layouts, local(): send_grads = jnp.zeros((EXPERTS * CAP, DOUT), jnp.float32).at[slot_place]...  45.7 us
    all_to_all x4, starting transfers between devices, local(): lax.all_to_all(slot_out.reshape(EXPERTS, CAP, DOUT), 'expert', split_axis...  44.2 us
    scatter x4, local copies, waits for them, and re-layouts, local(): send_rows = jnp.zeros((EXPERTS * CAP, D), jnp.float32).at[slot_place].set...  43.9 us
    psum x1, blocking collectives, local(): gate_grad = lax.psum(gate_local, ('dp', 'expert'))  41.1 us
  transfers between devices with their start and end apart: 43, of which 21 were waited for; matrix products, arithmetic and copies ran while one was open for 31% of the time, Pallas kernels for 0%

profile of v1, /device:TPU:0, one launch (start us, length us, event | category | flops | bytes accessed | tf_op | source)
XLA Modules:
  0.0 1444.1 jit_solution(13970313278706490471)
XLA Ops:
  78.6 18.3 %collective-permute-done.11 = f32[2,192,256]{2,1,0:T(8,128)S(1)} collective-permute-done((f32[2,192,256]{2,1,0:T(8,128)S(1)}, f32[2,192,256]{2,1,0:T(8,128)S(1)}, u32[]{:S(2)}, u32[]{:S(2)}) %collective-permute-start.11) | collective-permute-done | bytes 393248 | tf_op jit(solution)/shard_map/ppermute | solution.py:159
  105.3 11.5 all-to-all-start.1
  137.8 11.4 scatter_custom_fusion.2
  158.9 18.2 %collective-permute-done.15 = f32[2,192,256]{2,1,0:T(8,128)S(1)} collective-permute-done((f32[2,192,256]{2,1,0:T(8,128)S(1)}, f32[2,192,256]{2,1,0:T(8,128)S(1)}, u32[]{:S(2)}, u32[]{:S(2)}) %collective-permute-start.15) | collective-permute-done | bytes 393248 | tf_op jit(solution)/shard_map/ppermute | solution.py:159
  189.7 41.3 %collective-permute-done.17 = f32[2,192,256]{2,1,0:T(8,128)S(1)} collective-permute-done((f32[2,192,256]{2,1,0:T(8,128)S(1)}, f32[2,192,256]{2,1,0:T(8,128)S(1)}, u32[]{:S(2)}, u32[]{:S(2)}) %collective-permute-start.17) | collective-permute-done | bytes 393248 | tf_op jit(solution)/shard_map/ppermute | solution.py:159
  231.0 15.9 %collective-permute-done.18 = f32[2,192,256]{2,1,0:T(8,128)S(1)} collective-permute-done((f32[2,192,256]{2,1,0:T(8,128)S(1)}, f32[2,192,256]{2,1,0:T(8,128)S(1)}, u32[]{:S(2)}, u32[]{:S(2)}) %collective-permute-start.18) | collective-permute-done | bytes 393248 | tf_op jit(solution)/shard_map/ppermute | solution.py:159
  287.0 39.4 %collective-permute-done.22 = f32[2,192,256]{2,1,0:T(8,128)S(1)} collective-permute-done((f32[2,192,256]{2,1,0:T(8,128)S(1)}, f32[2,192,256]{2,1,0:T(8,128)S(1)}, u32[]{:S(2)}, u32[]{:S(2)}) %collective-permute-start.22) | collective-permute-done | bytes 393248 | tf_op jit(solution)/shard_map/ppermute | solution.py:159
  334.9 45.4 %collective-permute-done.24 = f32[2,192,256]{2,1,0:T(8,128)S(1)} collective-permute-done((f32[2,192,256]{2,1,0:T(8,128)S(1)}, f32[2,192,256]{2,1,0:T(8,128)S(1)}, u32[]{:S(2)}, u32[]{:S(2)}) %collective-permute-start.24) | collective-permute-done | bytes 393248 | tf_op jit(solution)/shard_map/ppermute | solution.py:159
  380.3 15.9 %collective-permute-done.25 = f32[2,192,256]{2,1,0:T(8,128)S(1)} collective-permute-done((f32[2,192,256]{2,1,0:T(8,128)S(1)}, f32[2,192,256]{2,1,0:T(8,128)S(1)}, u32[]{:S(2)}, u32[]{:S(2)}) %collective-permute-start.25) | collective-permute-done | bytes 393248 | tf_op jit(solution)/shard_map/ppermute | solution.py:159
  436.4 39.3 %collective-permute-done.1 = f32[2,192,256]{2,1,0:T(8,128)S(1)} collective-permute-done((f32[2,192,256]{2,1,0:T(8,128)S(1)}, f32[2,192,256]{2,1,0:T(8,128)S(1)}, u32[]{:S(2)}, u32[]{:S(2)}) %collective-permute-start.1) | collective-permute-done | bytes 393248 | tf_op jit(solution)/shard_map/ppermute | solution.py:159
  484.1 45.4 %collective-permute-done.3 = f32[2,192,256]{2,1,0:T(8,128)S(1)} collective-permute-done((f32[2,192,256]{2,1,0:T(8,128)S(1)}, f32[2,192,256]{2,1,0:T(8,128)S(1)}, u32[]{:S(2)}, u32[]{:S(2)}) %collective-permute-start.3) | collective-permute-done | bytes 393248 | tf_op jit(solution)/shard_map/ppermute | solution.py:159
  529.5 15.9 %collective-permute-done.4 = f32[2,192,256]{2,1,0:T(8,128)S(1)} collective-permute-done((f32[2,192,256]{2,1,0:T(8,128)S(1)}, f32[2,192,256]{2,1,0:T(8,128)S(1)}, u32[]{:S(2)}, u32[]{:S(2)}) %collective-permute-start.4) | collective-permute-done | bytes 393248 | tf_op jit(solution)/shard_map/ppermute | solution.py:159
  693.9 11.5 scatter_custom_fusion.7
  710.8 11.4 scatter_custom_fusion.6
  722.2 60.1 %all-to-all-done.10 = f32[16,192,256]{2,1,0:T(8,128)S(1)} async-done(((f32[16,192,256]{2,1,0:T(8,128)}), f32[16,192,256]{2,1,0:T(8,128)S(1)}, u32[]{:S(2)}, u32[]{:S(2)}) %all-to-all-start.10) | async-done | bytes 3145760 | tf_op jit(solution)/shard_map/all_to_all | solution.py:168
  788.5 11.4 scatter_custom_fusion.4
  799.9 60.1 %all-to-all-done.8 = f32[16,192,256]{2,1,0:T(8,128)} async-done(((f32[16,192,256]{2,1,0:T(8,128)}), f32[16,192,256]{2,1,0:T(8,128)}, u32[]{:S(2)}, u32[]{:S(2)}) %all-to-all-start.8) | async-done | bytes 3145760 | tf_op jit(solution)/shard_map/all_to_all | solution.py:168
  863.7 11.5 scatter_custom_fusion.5
  875.1 60.0 %all-to-all-done.4 = f32[16,192,256]{2,1,0:T(8,128)S(1)} async-done(((f32[16,192,256]{2,1,0:T(8,128)}), f32[16,192,256]{2,1,0:T(8,128)S(1)}, u32[]{:S(2)}, u32[]{:S(2)}) %all-to-all-start.4) | async-done | bytes 3145760 | tf_op jit(solution)/shard_map/all_to_all | solution.py:168
  952.8 60.8 %all-to-all-done.6 = f32[16,192,256]{2,1,0:T(8,128)} async-done(((f32[16,192,256]{2,1,0:T(8,128)}), f32[16,192,256]{2,1,0:T(8,128)}, u32[]{:S(2)}, u32[]{:S(2)}) %all-to-all-start.6) | async-done | bytes 3145760 | tf_op jit(solution)/shard_map/all_to_all | solution.py:168
  1029.2 59.7 %all-to-all-done.5 = f32[16,192,256]{2,1,0:T(8,128)S(1)} async-done(((f32[16,192,256]{2,1,0:T(8,128)}), f32[16,192,256]{2,1,0:T(8,128)S(1)}, u32[]{:S(2)}, u32[]{:S(2)}) %all-to-all-start.5) | async-done | bytes 3145760 | tf_op jit(solution)/shard_map/all_to_all | solution.py:177
  1105.3 59.8 %all-to-all-done.11 = f32[16,192,256]{2,1,0:T(8,128)} async-done(((f32[16,192,256]{2,1,0:T(8,128)}), f32[16,192,256]{2,1,0:T(8,128)}, u32[]{:S(2)}, u32[]{:S(2)}) %all-to-all-start.11) | async-done | bytes 3145760 | tf_op jit(solution)/shard_map/all_to_all | solution.py:177
  1239.3 41.1 %psum.7 = f32[256,40]{0,1:T(8,128)S(1)} all-reduce(f32[256,40]{0,1:T(8,128)S(1)} %fusion.258), channel_id=1, replica_groups=mesh['dp'=4,'expert'=8] {'dp','expert'}, use_global_device_ids=true, to_apply=%region_36.37 | all-reduce | flops 10240 | bytes 81920 | tf_op jit(solution)/shard_map/psum | solution.py:208
  1370.2 19.4 %reduce-scatter.6.cloned.1.call-done = f32[2,64,256]{2,1,0:T(8,128)} async-done(((f32[2,256,256]{2,1,0:T(8,128)}), f32[2,64,256]{2,1,0:T(8,128)}) %reduce-scatter.6.cloned.1.call-update) | async-done | bytes 131088 | tf_op jit(solution)/shard_map/reduce_scatter | solution.py:210
  (527 shorter events, 643.5 us)
Async XLA Ops:
  105.3 150.0 %all-to-all-start.1 = ((f32[16,192,256]{2,1,0:T(8,128)}), f32[16,192,256]{2,1,0:T(8,128)S(1)}, u32[]{:S(2)}, u32[]{:S(2)}) async-start(f32[16,192,256]{2,1,0:T(8,128)} %bitcast.392), calls=%async_computation.1 | async-start | bytes 6291456 | tf_op jit(solution)/shard_map/all_to_all | solution.py:165
  153.6 77.4 %collective-permute-start.17 = (f32[2,192,256]{2,1,0:T(8,128)S(1)}, f32[2,192,256]{2,1,0:T(8,128)S(1)}, u32[]{:S(2)}, u32[]{:S(2)}) collective-permute-start(f32[2,192,256]{2,1,0:T(8,128)S(1)} %get-tuple-element.51), channel_id=1, source_target_pairs={{0,4},{1,5},{2,6},{3,7},{4,0},{5,1},{6,2},{7,3},{8,12},{9,13},{10,... | collective-permute-start | bytes 1179656 | tf_op jit(solution)/shard_map/ppermute | solution.py:159
  156.2 90.8 %collective-permute-start.20 = (f32[2,192,256]{2,1,0:T(8,128)S(1)}, f32[2,192,256]{2,1,0:T(8,128)S(1)}, u32[]{:S(2)}, u32[]{:S(2)}) collective-permute-start(f32[2,192,256]{2,1,0:T(8,128)S(1)} %get-tuple-element.48), channel_id=1, source_target_pairs={{0,7},{1,6},{2,5},{3,4},{4,3},{5,2},{6,1},{7,0},{8,15},{9,14},{10,... | collective-permute-start | bytes 1179656 | tf_op jit(solution)/shard_map/ppermute | solution.py:159
  157.4 89.5 %collective-permute-start.18 = (f32[2,192,256]{2,1,0:T(8,128)S(1)}, f32[2,192,256]{2,1,0:T(8,128)S(1)}, u32[]{:S(2)}, u32[]{:S(2)}) collective-permute-start(f32[2,192,256]{2,1,0:T(8,128)S(1)} %get-tuple-element.50), channel_id=1, source_target_pairs={{0,5},{1,4},{2,7},{3,6},{4,1},{5,0},{6,3},{7,2},{8,13},{9,12},{10,... | collective-permute-start | bytes 1179656 | tf_op jit(solution)/shard_map/ppermute | solution.py:159
  177.1 69.8 %collective-permute-start.19 = (f32[2,192,256]{2,1,0:T(8,128)S(1)}, f32[2,192,256]{2,1,0:T(8,128)S(1)}, u32[]{:S(2)}, u32[]{:S(2)}) collective-permute-start(f32[2,192,256]{2,1,0:T(8,128)S(1)} %get-tuple-element.49), channel_id=1, source_target_pairs={{0,6},{1,7},{2,4},{3,5},{4,2},{5,3},{6,0},{7,1},{8,14},{9,15},{10,... | collective-permute-start | bytes 1179656 | tf_op jit(solution)/shard_map/ppermute | solution.py:159
  255.3 149.3 %all-to-all-start.2 = ((f32[16,192,256]{2,1,0:T(8,128)}), f32[16,192,256]{2,1,0:T(8,128)}, u32[]{:S(2)}, u32[]{:S(2)}) async-start(f32[16,192,256]{2,1,0:T(8,128)} %bitcast.396), calls=%async_computation.2 | async-start | bytes 6291456 | tf_op jit(solution)/shard_map/all_to_all | solution.py:165
  282.8 97.4 %collective-permute-start.24 = (f32[2,192,256]{2,1,0:T(8,128)S(1)}, f32[2,192,256]{2,1,0:T(8,128)S(1)}, u32[]{:S(2)}, u32[]{:S(2)}) collective-permute-start(f32[2,192,256]{2,1,0:T(8,128)S(1)} %get-tuple-element.59), channel_id=1, source_target_pairs={{0,4},{1,5},{2,6},{3,7},{4,0},{5,1},{6,2},{7,3},{8,12},{9,13},{10,... | collective-permute-start | bytes 1179656 | tf_op jit(solution)/shard_map/ppermute | solution.py:159
  284.3 111.9 %collective-permute-start.27 = (f32[2,192,256]{2,1,0:T(8,128)S(1)}, f32[2,192,256]{2,1,0:T(8,128)S(1)}, u32[]{:S(2)}, u32[]{:S(2)}) collective-permute-start(f32[2,192,256]{2,1,0:T(8,128)S(1)} %get-tuple-element.56), channel_id=1, source_target_pairs={{0,7},{1,6},{2,5},{3,4},{4,3},{5,2},{6,1},{7,0},{8,15},{9,14},{10,... | collective-permute-start | bytes 1179656 | tf_op jit(solution)/shard_map/ppermute | solution.py:159
  286.6 109.6 %collective-permute-start.25 = (f32[2,192,256]{2,1,0:T(8,128)S(1)}, f32[2,192,256]{2,1,0:T(8,128)S(1)}, u32[]{:S(2)}, u32[]{:S(2)}) collective-permute-start(f32[2,192,256]{2,1,0:T(8,128)S(1)} %get-tuple-element.58), channel_id=1, source_target_pairs={{0,5},{1,4},{2,7},{3,6},{4,1},{5,0},{6,3},{7,2},{8,13},{9,12},{10,... | collective-permute-start | bytes 1179656 | tf_op jit(solution)/shard_map/ppermute | solution.py:159
  404.5 149.2 %all-to-all-start.3 = ((f32[16,192,256]{2,1,0:T(8,128)}), f32[16,192,256]{2,1,0:T(8,128)}, u32[]{:S(2)}, u32[]{:S(2)}) async-start(f32[16,192,256]{2,1,0:T(8,128)} %bitcast.394), calls=%async_computation.3 | async-start | bytes 6291456 | tf_op jit(solution)/shard_map/all_to_all | solution.py:165
  432.2 97.3 %collective-permute-start.3 = (f32[2,192,256]{2,1,0:T(8,128)S(1)}, f32[2,192,256]{2,1,0:T(8,128)S(1)}, u32[]{:S(2)}, u32[]{:S(2)}) collective-permute-start(f32[2,192,256]{2,1,0:T(8,128)S(1)} %get-tuple-element.35), channel_id=1, source_target_pairs={{0,4},{1,5},{2,6},{3,7},{4,0},{5,1},{6,2},{7,3},{8,12},{9,13},{10,... | collective-permute-start | bytes 1179656 | tf_op jit(solution)/shard_map/ppermute | solution.py:159
  433.8 111.7 %collective-permute-start.6 = (f32[2,192,256]{2,1,0:T(8,128)S(1)}, f32[2,192,256]{2,1,0:T(8,128)S(1)}, u32[]{:S(2)}, u32[]{:S(2)}) collective-permute-start(f32[2,192,256]{2,1,0:T(8,128)S(1)} %get-tuple-element.32), channel_id=1, source_target_pairs={{0,7},{1,6},{2,5},{3,4},{4,3},{5,2},{6,1},{7,0},{8,15},{9,14},{10,... | collective-permute-start | bytes 1179656 | tf_op jit(solution)/shard_map/ppermute | solution.py:159
  436.0 109.4 %collective-permute-start.4 = (f32[2,192,256]{2,1,0:T(8,128)S(1)}, f32[2,192,256]{2,1,0:T(8,128)S(1)}, u32[]{:S(2)}, u32[]{:S(2)}) collective-permute-start(f32[2,192,256]{2,1,0:T(8,128)S(1)} %get-tuple-element.34), channel_id=1, source_target_pairs={{0,5},{1,4},{2,7},{3,6},{4,1},{5,0},{6,3},{7,2},{8,13},{9,12},{10,... | collective-permute-start | bytes 1179656 | tf_op jit(solution)/shard_map/ppermute | solution.py:159
  475.7 69.8 %collective-permute-start.5 = (f32[2,192,256]{2,1,0:T(8,128)S(1)}, f32[2,192,256]{2,1,0:T(8,128)S(1)}, u32[]{:S(2)}, u32[]{:S(2)}) collective-permute-start(f32[2,192,256]{2,1,0:T(8,128)S(1)} %get-tuple-element.33), channel_id=1, source_target_pairs={{0,6},{1,7},{2,4},{3,5},{4,2},{5,3},{6,0},{7,1},{8,14},{9,15},{10,... | collective-permute-start | bytes 1179656 | tf_op jit(solution)/shard_map/ppermute | solution.py:159
  553.8 120.5 %all-to-all-start = ((f32[16,192,256]{2,1,0:T(8,128)}), f32[16,192,256]{2,1,0:T(8,128)}, u32[]{:S(2)}, u32[]{:S(2)}) async-start(f32[16,192,256]{2,1,0:T(8,128)} %bitcast.395), calls=%async_computation | async-start | bytes 6291456 | tf_op jit(solution)/shard_map/all_to_all | solution.py:165
  705.4 76.9 %all-to-all-start.10 = ((f32[16,192,256]{2,1,0:T(8,128)}), f32[16,192,256]{2,1,0:T(8,128)S(1)}, u32[]{:S(2)}, u32[]{:S(2)}) async-start(f32[16,192,256]{2,1,0:T(8,128)} %bitcast.402), calls=%async_computation.10 | async-start | bytes 6291456 | tf_op jit(solution)/shard_map/all_to_all | solution.py:168
  784.0 76.0 %all-to-all-start.8 = ((f32[16,192,256]{2,1,0:T(8,128)}), f32[16,192,256]{2,1,0:T(8,128)}, u32[]{:S(2)}, u32[]{:S(2)}) async-start(f32[16,192,256]{2,1,0:T(8,128)} %bitcast.401), calls=%async_computation.8 | async-start | bytes 6291456 | tf_op jit(solution)/shard_map/all_to_all | solution.py:168
  860.0 75.1 %all-to-all-start.4 = ((f32[16,192,256]{2,1,0:T(8,128)}), f32[16,192,256]{2,1,0:T(8,128)S(1)}, u32[]{:S(2)}, u32[]{:S(2)}) async-start(f32[16,192,256]{2,1,0:T(8,128)} %bitcast.400), calls=%async_computation.4 | async-start | bytes 6291456 | tf_op jit(solution)/shard_map/all_to_all | solution.py:168
  936.9 76.7 %all-to-all-start.6 = ((f32[16,192,256]{2,1,0:T(8,128)}), f32[16,192,256]{2,1,0:T(8,128)}, u32[]{:S(2)}, u32[]{:S(2)}) async-start(f32[16,192,256]{2,1,0:T(8,128)} %bitcast.399), calls=%async_computation.6 | async-start | bytes 6291456 | tf_op jit(solution)/shard_map/all_to_all | solution.py:168
  1013.6 75.3 %all-to-all-start.5 = ((f32[16,192,256]{2,1,0:T(8,128)}), f32[16,192,256]{2,1,0:T(8,128)S(1)}, u32[]{:S(2)}, u32[]{:S(2)}) async-start(f32[16,192,256]{2,1,0:T(8,128)} %bitcast.397), calls=%async_computation.5 | async-start | bytes 6291456 | tf_op jit(solution)/shard_map/all_to_all | solution.py:177
  1088.9 76.2 %all-to-all-start.11 = ((f32[16,192,256]{2,1,0:T(8,128)}), f32[16,192,256]{2,1,0:T(8,128)}, u32[]{:S(2)}, u32[]{:S(2)}) async-start(f32[16,192,256]{2,1,0:T(8,128)} %bitcast.398), calls=%async_computation.11 | async-start | bytes 6291456 | tf_op jit(solution)/shard_map/all_to_all | solution.py:177
  1165.1 126.7 %all-to-all-start.9 = ((f32[16,192,256]{2,1,0:T(8,128)}), f32[16,192,256]{2,1,0:T(8,128)}, u32[]{:S(2)}, u32[]{:S(2)}) async-start(f32[16,192,256]{2,1,0:T(8,128)} %bitcast.393), calls=%async_computation.9 | async-start | bytes 6291456 | tf_op jit(solution)/shard_map/all_to_all | solution.py:177
  1291.7 133.9 %all-to-all-start.7 = ((f32[16,192,256]{2,1,0:T(8,128)}), f32[16,192,256]{2,1,0:T(8,128)}, u32[]{:S(2)}, u32[]{:S(2)}) async-start(f32[16,192,256]{2,1,0:T(8,128)} %bitcast.391), calls=%async_computation.7 | async-start | bytes 6291456 | tf_op jit(solution)/shard_map/all_to_all | solution.py:177
  1296.3 70.6 %reduce-scatter.10.cloned.1.call-start = ((), (), s32[]{:S(2)}) async-start(), calls=%async_computation.17 | async-start | bytes 327680
  (118 other events, 1733.2 us)
Sparse Core Ops, SparseCore 0:
  1306.8 25.2 reduce-scatter.9
  1336.1 25.9 reduce-scatter.7
  1364.9 24.7 reduce-scatter.5
